TPU v7x, 128 devices: a whole 4x4x4 slice. The times are simulated.
128 devices in a mesh: section: 2 (over y_hi), expert: 8 (over z, core), hid: 8 (over x, y_lo).
Axes of the slice: x: 4, y: 4 (y_hi: 2, y_lo: 2; y = y_hi * 2 + y_lo), z: 4, core: 2. Of those that a mesh axis runs over, the one named last changes fastest.
Arguments:
- saved_input: bfloat16 [2, 1024, 4096], P('section', 'expert', 'hid'), may hold values from -6 to 6
- cotangent: bfloat16 [2, 1024, 4096], P('section', 'expert', 'hid'), may hold values from -6 to 6
- next_input: bfloat16 [2, 1024, 4096], P('section', 'expert', 'hid'), may hold values from -6 to 6
- routes_saved: int32 [2, 1024, 2], P('section', 'expert'), may hold values from 0 to 7, all different within a row; in each aligned block of 128 rows (0 to 127, 128 to 255, ..., all dimensions but the last counted through in order) at most 48 rows name the same one
- routes_next: int32 [2, 1024, 2], P('section', 'expert'), may hold values from 0 to 7, all different within a row; in each aligned block of 128 rows (0 to 127, 128 to 255, ..., all dimensions but the last counted through in order) at most 48 rows name the same one
- norm_gain: float32 [2, 4096], P('section', 'hid'), may hold values from 0.1 to 1.9
- router: float32 [2, 4096, 8], P('section', 'hid'), may hold values from -0.18 to 0.18
- expert_gate: bfloat16 [2, 8, 4096, 7168], P('section', 'expert', None, 'hid'), may hold values from -0.09375 to 0.09375
- expert_up: bfloat16 [2, 8, 4096, 7168], P('section', 'expert', None, 'hid'), may hold values from -0.09375 to 0.09375
- expert_down: bfloat16 [2, 8, 7168, 4096], P('section', 'expert', 'hid'), may hold values from -0.0625 to 0.0625
Outputs:
- leaving: bfloat16 [2, 1024, 4096], P('section', 'expert', 'hid')
- arriving: bfloat16 [2, 1024, 4096], P('section', 'expert', 'hid')
Inputs may be any that keep to these rules, and one draw needn't show every extreme that they name: `routes_saved`: A token's two ids differ. In each aligned block of 128 tokens of a section no expert is named by more than 48 tokens, and some block names some expert exactly 48 times. `routes_next`: A token's two ids differ. In each aligned block of 128 tokens of a section no expert is named by more than 48 tokens, and some block names some expert exactly 48 times.
All inputs are finite; a program needn't handle non-finite values.
Results may differ from a plain program's by a relative error of at most 0.0052.
Values may be sent and summed in bfloat16 or wider, within the bound.
No kernel may reach another device: no remote copies, remote signals or barrier semaphores. Data moves between devices by JAX's collectives and lax.ppermute only.
A program may use at most 128 MiB of HBM per device.

v0:
```python
import jax
import jax.numpy as jnp
from jax import lax
from jax.sharding import PartitionSpec as P

EPSILON = 1e-05
HIGHEST = lax.Precision.HIGHEST
CONTRACT = (((1,), (1,)), ((), ()))


def partner(block, axis, bit):
    count = lax.axis_size(axis)
    route = []
    for low in range(count):
        high = low | 1 << bit
        if high != low and high < count:
            route += [(low, high), (high, low)]
    return lax.ppermute(block, axis, route)


def norm_terms(values, gain, table):
    squares = jnp.sum(values * values, axis=1)
    partial_value = jnp.dot(values * gain[None, :], table, precision=HIGHEST)
    return (squares, partial_value)


def finish_norm(values, squares, partial_value, gain, width):
    scale = lax.rsqrt(squares / width + EPSILON)
    normed = (values * scale[:, None] * gain[None, :]).astype(jnp.bfloat16)
    return (scale, normed, scale[:, None] * partial_value)


def placing(routes, logits, capacity):
    experts = logits.shape[1]
    tokens = routes.shape[0]
    labels = jnp.arange(experts, dtype=jnp.int32)
    flat_ids = routes.reshape(-1)
    onehot = (flat_ids[:, None] == labels[None, :]).astype(jnp.int32)
    ranked = jnp.cumsum(onehot, axis=0) - onehot
    places = jnp.sum(ranked * onehot, axis=1)
    targets = (flat_ids * capacity + places).reshape(tokens, 2)
    first_hit = (routes[:, 0:1] == labels[None, :]).astype(jnp.float32)
    second_hit = (routes[:, 1:2] == labels[None, :]).astype(jnp.float32)
    first_logit = jnp.sum(logits * first_hit, axis=1)
    second_logit = jnp.sum(logits * second_hit, axis=1)
    first_prob = jax.nn.sigmoid(first_logit - second_logit)
    second_prob = jax.nn.sigmoid(second_logit - first_logit)
    all_slots = jnp.arange(experts * capacity, dtype=jnp.int32)
    slot_map = jnp.any(targets[None, :, :] == all_slots[:, None, None], axis=2).astype(jnp.bfloat16)
    return (targets, first_prob, second_prob, first_hit - second_hit, slot_map)


def row_buffer(slot_map, rows):
    return jnp.dot(slot_map, rows, preferred_element_type=jnp.float32).astype(jnp.bfloat16)


def blend(rows, targets, first_prob, second_prob):
    return first_prob[:, None] * rows[targets[:, 0]] + second_prob[:, None] * rows[targets[:, 1]]


def add_products(matrices, pieces):
    gate_matrix, up_matrix, down_matrix = matrices
    saved_rows, cot_rows, next_rows = pieces
    gate_saved = jnp.dot(saved_rows, gate_matrix, preferred_element_type=jnp.float32)
    up_saved = jnp.dot(saved_rows, up_matrix, preferred_element_type=jnp.float32)
    grad_hidden = lax.dot_general(
        cot_rows, down_matrix, CONTRACT, preferred_element_type=jnp.float32
    )
    gate_next = jnp.dot(next_rows, gate_matrix, preferred_element_type=jnp.float32)
    up_next = jnp.dot(next_rows, up_matrix, preferred_element_type=jnp.float32)
    return (gate_saved, up_saved, grad_hidden, gate_next, up_next)


def per_device(
    saved_input,
    cotangent,
    next_input,
    routes_saved,
    routes_next,
    norm_gain,
    router,
    expert_gate,
    expert_up,
    expert_down,
):
    gain = norm_gain[0]
    table = router[0]
    gate_matrix = expert_gate[0, 0]
    up_matrix = expert_up[0, 0]
    down_matrix = expert_down[0, 0]
    matrices = (gate_matrix, up_matrix, down_matrix)
    width = gate_matrix.shape[0]
    cot_rows = cotangent[0]
    values_saved = saved_input[0].astype(jnp.float32)
    values_next = next_input[0].astype(jnp.float32)
    squares_saved, partial_saved = norm_terms(values_saved, gain, table)
    squares_next, partial_next = norm_terms(values_next, gain, table)
    squares_saved, partial_saved, squares_next, partial_next = lax.psum(
        (squares_saved, partial_saved, squares_next, partial_next), "hid"
    )
    scale_saved, normed_saved, logits_saved = finish_norm(
        values_saved, squares_saved, partial_saved, gain, width
    )
    scale_next, normed_next, logits_next = finish_norm(
        values_next, squares_next, partial_next, gain, width
    )
    tokens = values_saved.shape[0]
    experts = lax.axis_size("expert")
    capacity = 3 * tokens // experts
    targets_saved, first_saved, second_saved, diff_saved, map_saved = placing(
        routes_saved[0], logits_saved, capacity
    )
    targets_next, first_next, second_next, diff_next, map_next = placing(
        routes_next[0], logits_next, capacity
    )
    packed = (
        row_buffer(map_saved, normed_saved),
        row_buffer(map_saved, cot_rows),
        row_buffer(map_next, normed_next),
    )
    moved = (
        lax.all_to_all(packed[0], "expert", split_axis=0, concat_axis=0, tiled=True),
        lax.all_to_all(packed[1], "expert", split_axis=0, concat_axis=0, tiled=True),
        lax.all_to_all(packed[2], "expert", split_axis=0, concat_axis=0, tiled=True),
    )
    sums = add_products(
        matrices,
        (
            lax.all_gather(moved[0], "hid", axis=1, tiled=True),
            lax.all_gather(moved[1], "hid", axis=1, tiled=True),
            lax.all_gather(moved[2], "hid", axis=1, tiled=True),
        ),
    )
    gate_saved, up_saved, grad_hidden, gate_next, up_next = sums
    sig_saved = jax.nn.sigmoid(gate_saved)
    silu_saved = gate_saved * sig_saved
    hidden_saved = (silu_saved * up_saved).astype(jnp.bfloat16)
    dot_terms = jnp.sum(grad_hidden * hidden_saved.astype(jnp.float32), axis=1)
    row_dots = lax.psum(dot_terms, "hid")
    grad_gate = (
        grad_hidden * up_saved * (sig_saved * (1.0 + gate_saved * (1.0 - sig_saved)))
    ).astype(jnp.bfloat16)
    grad_up = (grad_hidden * silu_saved).astype(jnp.bfloat16)
    back_part = lax.dot_general(
        grad_gate, gate_matrix, CONTRACT, preferred_element_type=jnp.float32
    ) + lax.dot_general(grad_up, up_matrix, CONTRACT, preferred_element_type=jnp.float32)
    silu_next = gate_next * jax.nn.sigmoid(gate_next)
    hidden_next = (silu_next * up_next).astype(jnp.bfloat16)
    out_part = jnp.dot(hidden_next, down_matrix, preferred_element_type=jnp.float32)
    back_sum, out_sum = (
        lax.psum_scatter(back_part, "hid", scatter_dimension=1, tiled=True),
        lax.psum_scatter(out_part, "hid", scatter_dimension=1, tiled=True),
    )
    back_home, dots_home, out_home = (
        lax.all_to_all(back_sum, "expert", split_axis=0, concat_axis=0, tiled=True),
        lax.all_to_all(row_dots, "expert", split_axis=0, concat_axis=0, tiled=True),
        lax.all_to_all(out_sum, "expert", split_axis=0, concat_axis=0, tiled=True),
    )
    mixed_saved = blend(back_home, targets_saved, first_saved, second_saved)
    branch_next = blend(out_home, targets_next, first_next, second_next)
    forward_out = (values_next + branch_next).astype(jnp.bfloat16)
    grad_logit = (
        (dots_home[targets_saved[:, 0]] - dots_home[targets_saved[:, 1]])
        * first_saved
        * second_saved
    )
    grad_normed = mixed_saved + jnp.dot(
        grad_logit[:, None] * diff_saved, table.T, precision=HIGHEST
    )
    scaled_grad = grad_normed * gain[None, :]
    inner = lax.psum(jnp.sum(scaled_grad * values_saved, axis=1), "hid")
    cube = scale_saved * scale_saved * scale_saved
    grad_input = (
        cot_rows.astype(jnp.float32)
        + scale_saved[:, None] * scaled_grad
        - values_saved * cube[:, None] * (inner / width)[:, None]
    )
    grad_input = grad_input.astype(jnp.bfloat16)
    first_section = lax.axis_index("section") == 0
    outgoing = jnp.where(first_section, forward_out, grad_input)
    leaving = jnp.where(first_section, grad_input, forward_out)
    arriving = partner(outgoing, "section", 0)
    return (leaving[None], arriving[None])


def solution(mesh):
    placed = (
        P("section", "expert", "hid"),
        P("section", "expert", "hid"),
        P("section", "expert", "hid"),
        P("section", "expert", None),
        P("section", "expert", None),
        P("section", "hid"),
        P("section", "hid", None),
        P("section", "expert", None, "hid"),
        P("section", "expert", None, "hid"),
        P("section", "expert", "hid", None),
    )
    return jax.shard_map(
        per_device,
        mesh=mesh,
        in_specs=placed,
        out_specs=(P("section", "expert", "hid"), P("section", "expert", "hid")),
        check_vma=False,
    )
```

profile of v0, /device:TPU:0, one launch (start us, length us, event | category | flops | bytes accessed | tf_op | source)
XLA Modules:
  0.0 648.1 jit_solution(6616434694353465557)
XLA Ops:
  7.2 0.8 copy.58
  8.3 1.0 fusion.39
  9.4 19.8 %psum.42 = f32[128]{0:T(128)S(1)} all-reduce(f32[128]{0:T(128)S(1)} %fusion.39), channel_id=1, replica_groups=mesh['section'=2,'expert'=8,'hid'=8] {'hid'}, use_global_device_ids=true, to_apply=%region_1.0 | all-reduce | flops 128 | bytes 1024 | tf_op jit(solution)/shard_map/psum | solution.py:98
  29.2 0.6 reduce-window.14
  30.3 0.7 add_bitcast_fusion.1
  31.1 1.2 convolution_convert_fusion.1
  32.3 14.2 %all_to_all.72 = bf16[8,48,512]{2,1,0:T(8,128)(2,1)} all-to-all(bf16[8,48,512]{2,1,0:T(8,128)(2,1)S(1)} %bitcast.152), channel_id=1, replica_groups=mesh['section'=2,'expert'=8,'hid'=8] {'expert'}, dimensions={0} | all-to-all | bytes 786432 | tf_op jit(solution)/shard_map/all_to_all | solution.py:122
  46.6 0.2 convolution_convert_fusion.2
  46.8 12.0 %all_to_all.73 = bf16[8,48,512]{2,1,0:T(8,128)(2,1)} all-to-all(bf16[8,48,512]{2,1,0:T(8,128)(2,1)S(1)} %bitcast.150), channel_id=1, replica_groups=mesh['section'=2,'expert'=8,'hid'=8] {'expert'}, dimensions={0} | all-to-all | bytes 786432 | tf_op jit(solution)/shard_map/all_to_all | solution.py:123
  58.9 54.5 %all-gather.6.cloned.1.call-done = bf16[384,4096]{1,0:T(8,128)(2,1)} async-done(((bf16[384,512]{1,0:T(8,128)(2,1)}), bf16[384,4096]{1,0:T(8,128)(2,1)}) %all-gather.6.cloned.1.call-update) | async-done | bytes 3145744 | tf_op jit(solution)/shard_map/all_gather | solution.py:129
  113.5 9.0 %fusion.4 = f32[384,896]{1,0:T(8,128)S(1)} fusion(bf16[384,4096]{1,0:T(8,128)(2,1)} %all-gather.6.cloned.1.call-done, bf16[1,1,4096,896]{3,2,1,0:T(8,128)(2,1)} %param.17), kind=kOutput, calls=%fused_computation.10 | convolution fusion | flops 2818572288 | bytes 11862016 | tf_op jit(solution)/shard_map/dot_general | solution.py:64
  122.5 5.7 fusion.10
  128.2 58.1 %all-gather.4.cloned.1.call-done = bf16[384,4096]{1,0:T(8,128)(2,1)} async-done(((bf16[384,512]{1,0:T(8,128)(2,1)}), bf16[384,4096]{1,0:T(8,128)(2,1)}) %all-gather.4.cloned.1.call-update) | async-done | bytes 3145744 | tf_op jit(solution)/shard_map/all_gather | solution.py:130
  186.3 8.5 %multiply_reduce_fusion = (f32[384]{0:T(512)S(1)}, f32[384,896]{1,0:T(8,128)S(1)}) fusion(f32[384,896]{1,0:T(8,128)S(1)} %fusion.10, f32[384,896]{1,0:T(8,128)S(1)} %fusion.4, bf16[384,4096]{1,0:T(8,128)(2,1)} %all-gather.4.cloned.1.call-done, bf16[1,1,896,4096]{3,2,1,0:T(8,128)(2,1)} %param.19), kind=kOutput, calls=%fused_computation.24 | convolution fusion | flops 2821668352 | bytes 14616064 | tf_op jit(solution)/shard_map/dot_general | solution.py:66
  194.8 6.1 fusion.2
  200.9 10.1 %fusion.16 = f32[384,4096]{1,0:T(8,128)} fusion(f32[384,4096]{1,0:T(8,128)S(1)} %fusion.2, bf16[1,1,4096,896]{3,2,1,0:T(8,128)(2,1)} %param.18, f32[384,896]{1,0:T(8,128)S(1)} %get-tuple-element.30, f32[384,896]{1,0:T(8,128)S(1)} %fusion.4), kind=kOutput, calls=%fused_computation.22 | convolution fusion | flops 2822209536 | bytes 22675456 | tf_op jit(solution)/shard_map/dot_general | solution.py:146
  211.0 0.6 copy-done.5
  212.2 0.6 reduce-window.16
  213.6 0.3 fusion.47
  214.0 26.3 %all-reduce.1 = (f32[128,8]{0,1:T(8,128)S(1)}, f32[8,48,1]{1,0,2:T(8,128)}) all-reduce(f32[128,8]{0,1:T(8,128)S(1)} %fusion.47, f32[8,48,1]{1,0,2:T(8,128)S(1)} %all_to_all.57), channel_id=1, replica_groups=mesh['section'=2,'expert'=8,'hid'=8] {'hid'}, use_global_device_ids=true, to_apply=%region_2.0 | all-reduce | flops 1408 | bytes 11264 | tf_op jit(solution)/shard_map/psum | solution.py:98
  240.3 4.5 all-to-all-start.3
  245.0 5.0 all-to-all-done.3
  250.0 92.7 %reduce-scatter.3.cloned.1.call-done = f32[384,512]{1,0:T(8,128)} async-done(((f32[384,4096]{1,0:T(8,128)}), f32[384,512]{1,0:T(8,128)}) %reduce-scatter.3.cloned.1.call-update) | async-done | bytes 786448 | tf_op jit(solution)/shard_map/reduce_scatter | solution.py:151
  342.7 4.4 all-to-all-start.2
  347.3 0.3 fusion.54
  347.7 0.5 broadcast.217
  348.2 0.7 reduce.23
  349.0 1.3 gather_fusion.3
  350.2 1.3 gather_fusion.2
  351.5 8.8 %all-to-all-done.2 = f32[8,48,512]{2,1,0:T(8,128)S(1)} async-done(((f32[8,48,512]{2,1,0:T(8,128)}), f32[8,48,512]{2,1,0:T(8,128)S(1)}, u32[]{:S(2)}, u32[]{:S(2)}) %all-to-all-start.2) | async-done | bytes 786464 | tf_op jit(solution)/shard_map/all_to_all | solution.py:155
  360.3 0.8 gather_fusion.1
  361.1 0.8 gather_fusion
  361.8 0.5 fusion.45
  362.4 18.8 %all-reduce = (f32[128]{0:T(128)S(1)}, f32[128]{0:T(128)S(1)}, f32[128,8]{0,1:T(8,128)S(1)}) all-reduce(f32[128]{0:T(128)S(1)} %get-tuple-element.31, f32[128]{0:T(128)S(1)} %fusion.49, f32[128,8]{0,1:T(8,128)S(1)} %fusion.54), channel_id=1, replica_groups=mesh['section'=2,'expert'=8,'hid'=8] {'hid'}, use_global_device_ids=true, to_apply=%region_13.14 | all-reduce | flops 1280 | bytes 10240 | tf_op jit(solution)/shard_map/psum | solution.py:171
  381.1 0.3 convolution_convert_fusion
  381.5 12.0 %all_to_all.74 = bf16[8,48,512]{2,1,0:T(8,128)(2,1)} all-to-all(bf16[8,48,512]{2,1,0:T(8,128)(2,1)S(1)} %bitcast.151), channel_id=1, replica_groups=mesh['section'=2,'expert'=8,'hid'=8] {'expert'}, dimensions={0} | all-to-all | bytes 786432 | tf_op jit(solution)/shard_map/all_to_all | solution.py:124
  393.6 67.0 %all-gather.8.cloned.1.call-done = bf16[384,4096]{1,0:T(8,128)(2,1)} async-done(((bf16[384,512]{1,0:T(8,128)(2,1)}), bf16[384,4096]{1,0:T(8,128)(2,1)}) %all-gather.8.cloned.1.call-update) | async-done | bytes 3145744 | tf_op jit(solution)/shard_map/all_gather | solution.py:131
  460.6 8.0 %fusion = f32[384,896]{1,0:T(8,128)S(1)} fusion(bf16[384,4096]{1,0:T(8,128)(2,1)} %all-gather.8.cloned.1.call-done, bf16[1,1,4096,896]{3,2,1,0:T(8,128)(2,1)} %param.17), kind=kOutput, calls=%fused_computation.6 | convolution fusion | flops 2818572288 | bytes 11862016 | tf_op jit(solution)/shard_map/dot_general | solution.py:69
  468.6 15.4 %fusion.12 = f32[384,4096]{1,0:T(8,128)} fusion(bf16[1,1,896,4096]{3,2,1,0:T(8,128)(2,1)} %param.19, bf16[384,4096]{1,0:T(8,128)(2,1)} %all-gather.8.cloned.1.call-done, bf16[1,1,4096,896]{3,2,1,0:T(8,128)(2,1)} %param.18, f32[384,896]{1,0:T(8,128)S(1)} %fusion), kind=kOutput, calls=%fused_computation.18 | convolution fusion | flops 5639208960 | bytes 25493504 | tf_op jit(solution)/shard_map/dot_general | solution.py:149
  484.4 130.6 %reduce-scatter.5.cloned.1.call-done = f32[384,512]{1,0:T(8,128)} async-done(((f32[384,4096]{1,0:T(8,128)}), f32[384,512]{1,0:T(8,128)}) %reduce-scatter.5.cloned.1.call-update) | async-done | bytes 786448 | tf_op jit(solution)/shard_map/reduce_scatter | solution.py:152
  615.0 4.4 all-to-all-start.5
  619.7 12.9 %all-to-all-done.5 = f32[8,48,512]{2,1,0:T(8,128)S(1)} async-done(((f32[8,48,512]{2,1,0:T(8,128)}), f32[8,48,512]{2,1,0:T(8,128)S(1)}, u32[]{:S(2)}, u32[]{:S(2)}) %all-to-all-start.5) | async-done | bytes 786464 | tf_op jit(solution)/shard_map/all_to_all | solution.py:157
  632.6 0.8 gather_fusion.5
  633.4 0.8 gather_fusion.4
  634.3 2.8 collective-permute-start
  637.1 0.7 select_bitcast_fusion
  637.8 3.2 collective-permute-done
  641.0 0.7 copy.68
  (66 shorter events, 3.8 us)
Async XLA Ops:
  7.2 206.5 %copy-start = (f32[1,512,8]{1,2,0:T(8,128)S(1)}, f32[1,512,8]{1,2,0:T(8,128)}, u32[]{:S(2)}) copy-start(f32[1,512,8]{1,2,0:T(8,128)} %param.16) | copy-start | bytes 49156
  7.2 39.4 %copy-start.3 = (bf16[1,128,512]{2,1,0:T(8,128)(2,1)S(1)}, bf16[1,128,512]{2,1,0:T(8,128)(2,1)}, u32[]{:S(2)}) copy-start(bf16[1,128,512]{2,1,0:T(8,128)(2,1)} %param.11) | copy-start | bytes 393220
  7.2 106.3 %all-gather.6.cloned.1.call-start = ((), (), s32[]{:S(2)}) async-start(), calls=%async_computation.9 | async-start | bytes 3538944 | tf_op jit(solution)/shard_map/all_gather | solution.py:129
  46.5 139.8 %all-gather.4.cloned.1.call-start = ((), (), s32[]{:S(2)}) async-start(), calls=%async_computation.8 | async-start | bytes 3538944 | tf_op jit(solution)/shard_map/all_gather | solution.py:130
  58.9 283.9 %reduce-scatter.3.cloned.1.call-start = ((), (), s32[]{:S(2)}) async-start(), calls=%async_computation.10 | async-start | bytes 7077888 | tf_op jit(solution)/shard_map/reduce_scatter | solution.py:151
  113.5 9.0 %copy-start.6 = (bf16[384,4096]{1,0:T(8,128)(2,1)S(1)}, bf16[384,4096]{1,0:T(8,128)(2,1)}, u32[]{:S(2)}) copy-start(bf16[384,4096]{1,0:T(8,128)(2,1)} %all-gather.6.cloned.1.call-done) | copy-start | bytes 9437188
  211.0 0.7 copy-start.5
  211.0 2.7 copy-start.1
  211.0 2.7 copy-start.4
  211.6 135.6 %copy-start.2 = (bf16[1,128,512]{2,1,0:T(8,128)(2,1)S(1)}, bf16[1,128,512]{2,1,0:T(8,128)(2,1)}, u32[]{:S(2)}) copy-start(bf16[1,128,512]{2,1,0:T(8,128)(2,1)} %param.12) | copy-start | bytes 393220
  240.3 9.7 %all-to-all-start.3 = ((f32[8,48,1]{1,2,0:T(1,128)}), f32[8,48,1]{1,2,0:T(1,128)S(1)}, u32[]{:S(2)}, u32[]{:S(2)}) async-start(f32[8,48,1]{1,2,0:T(1,128)} %bitcast.18), calls=%async_computation.4 | async-start | bytes 8192 | tf_op jit(solution)/shard_map/all_to_all | solution.py:156
  342.7 17.6 %all-to-all-start.2 = ((f32[8,48,512]{2,1,0:T(8,128)}), f32[8,48,512]{2,1,0:T(8,128)S(1)}, u32[]{:S(2)}, u32[]{:S(2)}) async-start(f32[8,48,512]{2,1,0:T(8,128)} %bitcast.153), calls=%async_computation.3 | async-start | bytes 1572864 | tf_op jit(solution)/shard_map/all_to_all | solution.py:155
  347.2 113.5 %all-gather.8.cloned.1.call-start = ((), (), s32[]{:S(2)}) async-start(), calls=%async_computation.11 | async-start | bytes 3538944 | tf_op jit(solution)/shard_map/all_gather | solution.py:131
  393.5 221.5 %reduce-scatter.5.cloned.1.call-start = ((), (), s32[]{:S(2)}) async-start(), calls=%async_computation.12 | async-start | bytes 7077888 | tf_op jit(solution)/shard_map/reduce_scatter | solution.py:152
  615.0 17.6 %all-to-all-start.5 = ((f32[8,48,512]{2,1,0:T(8,128)}), f32[8,48,512]{2,1,0:T(8,128)S(1)}, u32[]{:S(2)}, u32[]{:S(2)}) async-start(f32[8,48,512]{2,1,0:T(8,128)} %bitcast.154), calls=%async_computation.7 | async-start | bytes 1572864 | tf_op jit(solution)/shard_map/all_to_all | solution.py:157
  634.3 6.6 %collective-permute-start = (bf16[128,512]{1,0:T(8,128)(2,1)S(1)}, bf16[128,512]{1,0:T(8,128)(2,1)S(1)}, u32[]{:S(2)}, u32[]{:S(2)}) collective-permute-start(bf16[128,512]{1,0:T(8,128)(2,1)S(1)} %get-tuple-element.19), channel_id=1, source_target_pairs={{0,64},{64,0},{1,65},{65,1},{2,66},{66,2},{3,67},{67,3},{4,68},{68... | collective-permute-start | bytes 393224 | tf_op jit(solution)/shard_map/ppermute | solution.py:18
Sparse Core Ops, SparseCore 0:
  46.6 66.7 all-gather.5
  115.1 71.1 all-gather.3
  211.1 131.5 reduce-scatter.2
  393.7 66.9 all-gather.7
  484.2 130.8 reduce-scatter.4
where the time goes:
time: 649 us; the launch traced here: 648 us
  waiting for transfers between devices  433 us (67%)
  blocking collectives  103 us (16%)
  matrix products  65.6 us (10%)
  starting transfers between devices  16.3 us (3%)
  between operations  14.1 us (2%)
  local copies, waits for them, and re-layouts  10.5 us (2%)
    reduce_scatter x1, waiting for transfers between devices, per_device(): lax.psum_scatter(out_part, 'hid', scatter_dimension=1, tiled=True)  131 us
    reduce_scatter x1, waiting for transfers between devices, per_device(): lax.psum_scatter(back_part, 'hid', scatter_dimension=1, tiled=True)  92.7 us
    all_gather x1, waiting for transfers between devices, per_device(): lax.all_gather(moved[2], 'hid', axis=1, tiled=True)  67 us
    all_gather x1, waiting for transfers between devices, per_device(): lax.all_gather(moved[1], 'hid', axis=1, tiled=True)  58.1 us
    all_gather x1, waiting for transfers between devices, per_device(): lax.all_gather(moved[0], 'hid', axis=1, tiled=True)  54.5 us
    psum x2, blocking collectives, per_device(): lax.psum((squares_saved, partial_saved, squares_next, partial_next), 'hid')  46.2 us
    psum x1, blocking collectives, per_device(): inner = lax.psum(jnp.sum(scaled_grad * values_saved, axis=1), 'hid')  18.8 us
    dot_general x1, matrix products, per_device(): jnp.dot(hidden_next, down_matrix, preferred_element_type=jnp.float32)  15.4 us
  transfers between devices with their start and end apart: 9, of which 9 were waited for; matrix products, arithmetic and copies ran while one was open for 4% of the time, Pallas kernels for 0%

commit v1 on v0

--- a/solution.py
+++ b/solution.py
@@ -126,7 +126,9 @@
     sums = add_products(
         matrices,
         (
-            lax.all_gather(moved[0], "hid", axis=1, tiled=True),
+            jnp.concatenate(
+                lax.all_to_all(jnp.stack([moved[0]] * lax.axis_size("hid")), "hid", 0, 0), axis=1
+            ),
             lax.all_gather(moved[1], "hid", axis=1, tiled=True),
             lax.all_gather(moved[2], "hid", axis=1, tiled=True),
         ),

time: 649 us -> 604 us (0.931)
  waiting for transfers between devices: 433 us -> 341 us
  blocking collectives: 103 us -> 147 us
    all_gather x1 -> x0, waiting for transfers between devices: 54.5 us -> none  [per_device(): lax.all_gather(moved[0], 'hid', axis=1, tiled=True)]
    all_to_all x1, blocking collectives: 12 us -> 56.7 us  [per_device(): lax.all_to_all(jnp.stack([moved[0]] * lax.axis_size('hid')), 'hid', 0, 0)]
    all_gather x1, waiting for transfers between devices: 58.1 us -> 21 us  [per_device(): lax.all_gather(moved[1], 'hid', axis=1, tiled=True)]
  transfers between devices with their start and end apart: 9 -> 9, of which waited for: 9 -> 8; matrix products, arithmetic and copies ran while one was open for 4% -> 3% of each run, Pallas kernels for 0% -> 0%
where the time goes in v1:
time: 604 us
  waiting for transfers between devices  341 us (56%)
  blocking collectives  147 us (24%)
  matrix products  60.8 us (10%)
  starting transfers between devices  22.1 us (4%)
  between operations  14.1 us (2%)
  local copies, waits for them, and re-layouts  14 us (2%)
    reduce_scatter x1, waiting for transfers between devices, per_device(): lax.psum_scatter(out_part, 'hid', scatter_dimension=1, tiled=True)  131 us
    reduce_scatter x1, waiting for transfers between devices, per_device(): lax.psum_scatter(back_part, 'hid', scatter_dimension=1, tiled=True)  92.7 us
    all_gather x1, waiting for transfers between devices, per_device(): lax.all_gather(moved[2], 'hid', axis=1, tiled=True)  67 us
    all_to_all x1, blocking collectives, per_device(): lax.all_to_all(jnp.stack([moved[0]] * lax.axis_size('hid')), 'hid', 0, 0)  56.7 us
    psum x2, blocking collectives, per_device(): lax.psum((squares_saved, partial_saved, squares_next, partial_next), 'hid')  45.9 us
    all_gather x1, waiting for transfers between devices, per_device(): lax.all_gather(moved[1], 'hid', axis=1, tiled=True)  21 us
    psum x1, blocking collectives, per_device(): inner = lax.psum(jnp.sum(scaled_grad * values_saved, axis=1), 'hid')  18.8 us
    dot_general x1, matrix products, per_device(): jnp.dot(hidden_next, down_matrix, preferred_element_type=jnp.float32)  15.8 us
  transfers between devices with their start and end apart: 9, of which 8 were waited for; matrix products, arithmetic and copies ran while one was open for 3% of the time, Pallas kernels for 0%

profile of v1, /device:TPU:0, one launch (start us, length us, event | category | flops | bytes accessed | tf_op | source)
XLA Modules:
  0.0 603.7 jit_solution(18177613703360127737)
XLA Ops:
  7.2 0.8 copy.62
  8.3 0.6 reduce-window.14
  9.5 0.7 add_bitcast_fusion.1
  10.2 1.9 convolution_convert_fusion.2
  12.1 5.7 all-to-all-start
  17.9 19.7 %psum.42 = f32[128]{0:T(128)S(1)} all-reduce(f32[128]{0:T(128)S(1)} %fusion.39), channel_id=1, replica_groups=mesh['section'=2,'expert'=8,'hid'=8] {'hid'}, use_global_device_ids=true, to_apply=%region_1.0 | all-reduce | flops 128 | bytes 1024 | tf_op jit(solution)/shard_map/psum | solution.py:98
  37.8 0.3 convolution_convert_fusion.1
  38.1 13.6 %all_to_all.74 = bf16[8,48,512]{2,1,0:T(8,128)(2,1)} all-to-all(bf16[8,48,512]{2,1,0:T(8,128)(2,1)S(1)} %bitcast.159), channel_id=1, replica_groups=mesh['section'=2,'expert'=8,'hid'=8] {'expert'}, dimensions={0} | all-to-all | bytes 786432 | tf_op jit(solution)/shard_map/all_to_all | solution.py:122
  51.7 1.9 copy.66
  53.6 1.4 stack.5
  55.1 56.7 %all_to_all.75 = bf16[8,384,512]{1,2,0:T(8,128)(2,1)S(1)} all-to-all(bf16[8,384,512]{1,2,0:T(8,128)(2,1)S(1)} %stack.5), channel_id=1, replica_groups=mesh['section'=2,'expert'=8,'hid'=8] {'hid'}, dimensions={0} | all-to-all | bytes 6291456 | tf_op jit(solution)/shard_map/all_to_all | solution.py:130
  111.8 4.6 fusion.4
  116.4 3.4 fusion.10
  119.8 21.0 %all-gather.3.cloned.1.call-done = bf16[384,4096]{1,0:T(8,128)(2,1)} async-done(((bf16[384,512]{1,0:T(8,128)(2,1)}), bf16[384,4096]{1,0:T(8,128)(2,1)}) %all-gather.3.cloned.1.call-update) | async-done | bytes 3145744 | tf_op jit(solution)/shard_map/all_gather | solution.py:132
  140.8 8.7 %multiply_reduce_fusion = (f32[384]{0:T(512)S(1)}, f32[384,896]{1,0:T(8,128)S(1)}) fusion(f32[384,896]{1,0:T(8,128)S(1)} %fusion.10, f32[384,896]{1,0:T(8,128)S(1)} %copy-done.3, bf16[384,4096]{1,0:T(8,128)(2,1)} %all-gather.3.cloned.1.call-done, bf16[1,1,896,4096]{3,2,1,0:T(8,128)(2,1)} %param.19), kind=kOutput, calls=%fused_computation.24 | convolution fusion | flops 2821668352 | bytes 14616064 | tf_op jit(solution)/shard_map/dot_general | solution.py:66
  149.5 6.1 %fusion.2 = f32[384,4096]{1,0:T(8,128)S(1)} fusion(bf16[1,1,4096,896]{3,2,1,0:T(8,128)(2,1)} %param.17, f32[384,896]{1,0:T(8,128)S(1)} %copy-done.3, f32[384,896]{1,0:T(8,128)S(1)} %get-tuple-element.30, f32[384,896]{1,0:T(8,128)S(1)} %fusion.10), kind=kOutput, calls=%fused_computation.8 | convolution fusion | flops 2822012928 | bytes 17760256 | tf_op jit(solution)/shard_map/dot_general | solution.py:146
  155.6 10.1 %fusion.16 = f32[384,4096]{1,0:T(8,128)} fusion(f32[384,4096]{1,0:T(8,128)S(1)} %fusion.2, bf16[1,1,4096,896]{3,2,1,0:T(8,128)(2,1)} %param.18, f32[384,896]{1,0:T(8,128)S(1)} %get-tuple-element.30, f32[384,896]{1,0:T(8,128)S(1)} %copy-done.3), kind=kOutput, calls=%fused_computation.22 | convolution fusion | flops 2822209536 | bytes 22675456 | tf_op jit(solution)/shard_map/dot_general | solution.py:148
  165.7 0.7 copy-done.6
  166.9 0.6 reduce-window.16
  168.7 26.2 %all-reduce.1 = (f32[128,8]{0,1:T(8,128)S(1)}, f32[8,48,1]{1,0,2:T(8,128)}) all-reduce(f32[128,8]{0,1:T(8,128)S(1)} %fusion.47, f32[8,48,1]{1,0,2:T(8,128)S(1)} %all_to_all.58), channel_id=1, replica_groups=mesh['section'=2,'expert'=8,'hid'=8] {'hid'}, use_global_device_ids=true, to_apply=%region_2.0 | all-reduce | flops 1408 | bytes 11264 | tf_op jit(solution)/shard_map/psum | solution.py:98
  194.9 4.5 all-to-all-start.4
  199.5 5.0 all-to-all-done.4
  204.5 92.7 %reduce-scatter.3.cloned.1.call-done = f32[384,512]{1,0:T(8,128)} async-done(((f32[384,4096]{1,0:T(8,128)}), f32[384,512]{1,0:T(8,128)}) %reduce-scatter.3.cloned.1.call-update) | async-done | bytes 786448 | tf_op jit(solution)/shard_map/reduce_scatter | solution.py:153
  297.2 4.4 all-to-all-start.3
  302.1 0.3 fusion.54
  302.4 0.5 broadcast.218
  302.9 0.7 reduce.23
  303.7 1.3 gather_fusion.3
  305.0 1.3 gather_fusion.2
  306.3 8.6 %all-to-all-done.3 = f32[8,48,512]{2,1,0:T(8,128)S(1)} async-done(((f32[8,48,512]{2,1,0:T(8,128)}), f32[8,48,512]{2,1,0:T(8,128)S(1)}, u32[]{:S(2)}, u32[]{:S(2)}) %all-to-all-start.3) | async-done | bytes 786464 | tf_op jit(solution)/shard_map/all_to_all | solution.py:157
  314.8 0.8 gather_fusion.1
  315.6 0.8 gather_fusion
  316.3 0.5 fusion.45
  316.9 18.8 %all-reduce = (f32[128]{0:T(128)S(1)}, f32[128]{0:T(128)S(1)}, f32[128,8]{0,1:T(8,128)S(1)}) all-reduce(f32[128]{0:T(128)S(1)} %get-tuple-element.31, f32[128]{0:T(128)S(1)} %fusion.49, f32[128,8]{0,1:T(8,128)S(1)} %fusion.54), channel_id=1, replica_groups=mesh['section'=2,'expert'=8,'hid'=8] {'hid'}, use_global_device_ids=true, to_apply=%region_13.14 | all-reduce | flops 1280 | bytes 10240 | tf_op jit(solution)/shard_map/psum | solution.py:173
  335.6 0.3 convolution_convert_fusion
  336.0 12.0 %all_to_all.76 = bf16[8,48,512]{2,1,0:T(8,128)(2,1)} all-to-all(bf16[8,48,512]{2,1,0:T(8,128)(2,1)S(1)} %bitcast.160), channel_id=1, replica_groups=mesh['section'=2,'expert'=8,'hid'=8] {'expert'}, dimensions={0} | all-to-all | bytes 786432 | tf_op jit(solution)/shard_map/all_to_all | solution.py:124
  348.1 67.0 %all-gather.5.cloned.1.call-done = bf16[384,4096]{1,0:T(8,128)(2,1)} async-done(((bf16[384,512]{1,0:T(8,128)(2,1)}), bf16[384,4096]{1,0:T(8,128)(2,1)}) %all-gather.5.cloned.1.call-update) | async-done | bytes 3145744 | tf_op jit(solution)/shard_map/all_gather | solution.py:133
  415.1 8.5 %fusion = f32[384,896]{1,0:T(8,128)} fusion(bf16[384,4096]{1,0:T(8,128)(2,1)} %all-gather.5.cloned.1.call-done, bf16[1,1,4096,896]{3,2,1,0:T(8,128)(2,1)} %param.17), kind=kOutput, calls=%fused_computation.6 | convolution fusion | flops 2818572288 | bytes 11862016 | tf_op jit(solution)/shard_map/dot_general | solution.py:69
  423.7 15.8 %fusion.12 = f32[384,4096]{1,0:T(8,128)} fusion(bf16[1,1,896,4096]{3,2,1,0:T(8,128)(2,1)} %param.19, bf16[384,4096]{1,0:T(8,128)(2,1)} %all-gather.5.cloned.1.call-done, bf16[1,1,4096,896]{3,2,1,0:T(8,128)(2,1)} %param.18, f32[384,896]{1,0:T(8,128)} %fusion), kind=kOutput, calls=%fused_computation.18 | convolution fusion | flops 5639208960 | bytes 25493504 | tf_op jit(solution)/shard_map/dot_general | solution.py:151
  439.8 130.6 %reduce-scatter.5.cloned.1.call-done = f32[384,512]{1,0:T(8,128)} async-done(((f32[384,4096]{1,0:T(8,128)}), f32[384,512]{1,0:T(8,128)}) %reduce-scatter.5.cloned.1.call-update) | async-done | bytes 786448 | tf_op jit(solution)/shard_map/reduce_scatter | solution.py:154
  570.5 4.4 all-to-all-start.6
  575.1 12.9 %all-to-all-done.6 = f32[8,48,512]{2,1,0:T(8,128)S(1)} async-done(((f32[8,48,512]{2,1,0:T(8,128)}), f32[8,48,512]{2,1,0:T(8,128)S(1)}, u32[]{:S(2)}, u32[]{:S(2)}) %all-to-all-start.6) | async-done | bytes 786464 | tf_op jit(solution)/shard_map/all_to_all | solution.py:159
  588.0 0.8 gather_fusion.5
  588.8 0.8 gather_fusion.4
  589.9 2.8 collective-permute-start
  592.7 0.7 select_bitcast_fusion
  593.4 3.2 collective-permute-done
  596.5 0.7 copy.73
  (77 shorter events, 4.5 us)
Async XLA Ops:
  7.2 161.2 %copy-start = (f32[1,512,8]{1,2,0:T(8,128)S(1)}, f32[1,512,8]{1,2,0:T(8,128)}, u32[]{:S(2)}) copy-start(f32[1,512,8]{1,2,0:T(8,128)} %param.16) | copy-start | bytes 49156
  7.2 10.6 %copy-start.1 = (bf16[1,128,512]{2,1,0:T(8,128)(2,1)S(1)}, bf16[1,128,512]{2,1,0:T(8,128)(2,1)}, u32[]{:S(2)}) copy-start(bf16[1,128,512]{2,1,0:T(8,128)(2,1)} %param.10) | copy-start | bytes 393220
  7.2 30.6 %copy-start.5 = (f32[1,512]{1,0:T(1,128)S(1)}, f32[1,512]{1,0:T(1,128)}, u32[]{:S(2)}) copy-start(f32[1,512]{1,0:T(1,128)} %param.15) | copy-start | bytes 6148
  12.1 99.7 %slice-start = ((s8[7340032]{0:T(1024)(128)(4,1)}), s8[3145728]{0:T(1024)(128)(4,1)S(1)}, s32[]{:S(2)}) async-start(s8[7340032]{0:T(1024)(128)(4,1)} %bitcast.150), calls=%async_computation.13 | async-start | bytes 6291456
  12.1 25.5 %all-to-all-start = ((bf16[8,48,512]{2,1,0:T(8,128)(2,1)}), bf16[8,48,512]{2,1,0:T(8,128)(2,1)}, u32[]{:S(2)}, u32[]{:S(2)}) async-start(bf16[8,48,512]{2,1,0:T(8,128)(2,1)} %bitcast.157), calls=%async_computation | async-start | bytes 786432 | tf_op jit(solution)/shard_map/all_to_all | solution.py:123
  17.8 123.0 %all-gather.3.cloned.1.call-start = ((), (), s32[]{:S(2)}) async-start(), calls=%async_computation.9 | async-start | bytes 3538944 | tf_op jit(solution)/shard_map/all_gather | solution.py:132
  37.7 259.6 %reduce-scatter.3.cloned.1.call-start = ((), (), s32[]{:S(2)}) async-start(), calls=%async_computation.10 | async-start | bytes 7077888 | tf_op jit(solution)/shard_map/reduce_scatter | solution.py:153
  53.6 58.1 %slice-start.1 = ((s8[7340032]{0:T(1024)(128)(4,1)}), s8[4194304]{0:T(1024)(128)(4,1)S(1)}, s32[]{:S(2)}) async-start(s8[7340032]{0:T(1024)(128)(4,1)} %bitcast.150), calls=%async_computation.14 | async-start | bytes 8388608
  55.1 61.3 %slice-start.2 = ((s8[7340032]{0:T(1024)(128)(4,1)}), s8[4194304]{0:T(1024)(128)(4,1)S(1)}, s32[]{:S(2)}) async-start(s8[7340032]{0:T(1024)(128)(4,1)} %bitcast.152), calls=%async_computation.15 | async-start | bytes 8388608
  111.8 4.6 slice-start.3
  116.4 24.4 %copy-start.3 = (f32[384,896]{1,0:T(8,128)S(1)}, f32[384,896]{1,0:T(8,128)}, u32[]{:S(2)}) copy-start(f32[384,896]{1,0:T(8,128)} %fusion.4) | copy-start | bytes 4128772
  165.7 0.7 copy-start.6
  166.4 135.6 %copy-start.2 = (bf16[1,128,512]{2,1,0:T(8,128)(2,1)S(1)}, bf16[1,128,512]{2,1,0:T(8,128)(2,1)}, u32[]{:S(2)}) copy-start(bf16[1,128,512]{2,1,0:T(8,128)(2,1)} %param.12) | copy-start | bytes 393220
  194.9 9.7 %all-to-all-start.4 = ((f32[8,48,1]{1,2,0:T(1,128)}), f32[8,48,1]{1,2,0:T(1,128)S(1)}, u32[]{:S(2)}, u32[]{:S(2)}) async-start(f32[8,48,1]{1,2,0:T(1,128)} %bitcast.21), calls=%async_computation.5 | async-start | bytes 8192 | tf_op jit(solution)/shard_map/all_to_all | solution.py:158
  297.2 17.6 %all-to-all-start.3 = ((f32[8,48,512]{2,1,0:T(8,128)}), f32[8,48,512]{2,1,0:T(8,128)S(1)}, u32[]{:S(2)}, u32[]{:S(2)}) async-start(f32[8,48,512]{2,1,0:T(8,128)} %bitcast.161), calls=%async_computation.4 | async-start | bytes 1572864 | tf_op jit(solution)/shard_map/all_to_all | solution.py:157
  301.7 113.5 %all-gather.5.cloned.1.call-start = ((), (), s32[]{:S(2)}) async-start(), calls=%async_computation.11 | async-start | bytes 3538944 | tf_op jit(solution)/shard_map/all_gather | solution.py:133
  348.0 222.4 %reduce-scatter.5.cloned.1.call-start = ((), (), s32[]{:S(2)}) async-start(), calls=%async_computation.12 | async-start | bytes 7077888 | tf_op jit(solution)/shard_map/reduce_scatter | solution.py:154
  570.5 17.6 %all-to-all-start.6 = ((f32[8,48,512]{2,1,0:T(8,128)}), f32[8,48,512]{2,1,0:T(8,128)S(1)}, u32[]{:S(2)}, u32[]{:S(2)}) async-start(f32[8,48,512]{2,1,0:T(8,128)} %bitcast.162), calls=%async_computation.8 | async-start | bytes 1572864 | tf_op jit(solution)/shard_map/all_to_all | solution.py:159
  588.8 0.9 copy-start.4
  589.9 6.6 %collective-permute-start = (bf16[128,512]{1,0:T(8,128)(2,1)S(1)}, bf16[128,512]{1,0:T(8,128)(2,1)S(1)}, u32[]{:S(2)}, u32[]{:S(2)}) collective-permute-start(bf16[128,512]{1,0:T(8,128)(2,1)S(1)} %get-tuple-element.19), channel_id=1, source_target_pairs={{0,64},{64,0},{1,65},{65,1},{2,66},{66,2},{3,67},{67,3},{4,68},{68... | collective-permute-start | bytes 393224 | tf_op jit(solution)/shard_map/ppermute | solution.py:18
Sparse Core Ops, SparseCore 0:
  37.8 102.9 all-gather.2
  165.8 131.3 reduce-scatter.2
  348.2 66.9 all-gather.4
  439.6 130.8 reduce-scatter.4
